TPU v7x, 32 devices: a whole 2x2x4 slice. The times are simulated.
32 devices in a mesh: dp: 4 (over y, x), row: 4 (over z), col: 2 (over core).
Axes of the slice: x: 2, y: 2, z: 4, core: 2. Of those that a mesh axis runs over, the one named last changes fastest.
Arguments:
- image: bfloat16 [4, 256, 96, 256], P('dp', None, 'row', 'col'), may hold values from -6 to 6
- cotangent: bfloat16 [4, 256, 96, 256], P('dp', None, 'row', 'col'), may hold values from -6 to 6
- w_reduce: bfloat16 [256, 64], replicated, may hold values from -0.375 to 0.375
- w_spatial: bfloat16 [3, 3, 64, 64], replicated, may hold values from -0.25 to 0.25
- w_expand: bfloat16 [64, 256], replicated, may hold values from -0.75 to 0.75
Outputs:
- grad_image: bfloat16 [4, 256, 96, 256], P('dp', None, 'row', 'col')
- grad_reduce: float32 [256, 64], replicated
- grad_spatial: float32 [3, 3, 64, 64], replicated
- grad_expand: float32 [64, 256], replicated
All inputs are finite; a program needn't handle non-finite values.
Results may differ from a plain program's by a relative error of at most 0.0061.
Values may be sent and summed in bfloat16 or wider, within the bound.
A program may use at most 64 MiB of HBM per device.

v0:
```python
import jax
import jax.numpy as jnp
from jax import lax
from jax.sharding import PartitionSpec as P

GELU_C = 0.7978845608028654
GELU_K = 0.044715


def padded_2(block, sides, width):
    for axis, dim in sides:
        count = lax.axis_size(axis)
        forward = [(i, i + 1) for i in range(count - 1)]
        backward = [(target, source) for source, target in forward]
        low = lax.ppermute(
            lax.slice_in_dim(block, block.shape[dim] - width, None, axis=dim), axis, forward
        )
        high = lax.ppermute(lax.slice_in_dim(block, 0, width, axis=dim), axis, backward)
        block = jnp.concatenate([low, block, high], axis=dim)
    return block


def gelu(v):
    t = jnp.tanh(GELU_C * (v + GELU_K * v * v * v))
    return 0.5 * v * (1.0 + t)


def slope(v):
    t = jnp.tanh(GELU_C * (v + GELU_K * v * v * v))
    return 0.5 * (1.0 + t) + 0.5 * v * (1.0 - t * t) * GELU_C * (1.0 + 3.0 * GELU_K * v * v)


def stacked_taps(padded, height, width, flipped):
    pieces = []
    for row_k in range(3):
        for col_k in range(3):
            if flipped:
                pieces.append(
                    padded[:, 2 - row_k : 2 - row_k + height, 2 - col_k : 2 - col_k + width]
                )
            else:
                pieces.append(padded[:, row_k : row_k + height, col_k : col_k + width])
    return jnp.concatenate(pieces, axis=0)


def body(image, cotangent, w_reduce, w_spatial, w_expand):
    feats = image[0]
    upstream = cotangent[0]
    channels, height, width = feats.shape
    inner = w_reduce.shape[1]
    pixels = height * width * lax.axis_size("dp") * lax.axis_size("row") * lax.axis_size("col")
    scale = float(pixels) ** (-0.5)
    f32 = jnp.float32
    pre_one = jnp.einsum("chw,cm->mhw", feats, w_reduce, preferred_element_type=f32)
    hidden_one = gelu(pre_one).astype(jnp.bfloat16)
    pad_one = padded_2(hidden_one, (("row", 1), ("col", 2)), 1)
    patches = stacked_taps(pad_one, height, width, False)
    spatial_flat = w_spatial.reshape(9 * inner, inner)
    pre_two = jnp.einsum("khw,kd->dhw", patches, spatial_flat, preferred_element_type=f32)
    hidden_two = gelu(pre_two).astype(jnp.bfloat16)
    total = jnp.einsum(
        "mhw,mc->chw", hidden_two, w_expand, preferred_element_type=f32
    ) + feats.astype(f32)
    top = (upstream.astype(f32) * slope(total)).astype(jnp.bfloat16)
    grad_expand = jnp.einsum("mhw,chw->mc", hidden_two, top, preferred_element_type=f32) * scale
    back_two = (
        jnp.einsum("chw,mc->mhw", top, w_expand, preferred_element_type=f32) * slope(pre_two)
    ).astype(jnp.bfloat16)
    pad_back = padded_2(back_two, (("row", 1), ("col", 2)), 1)
    grad_spatial = (
        jnp.einsum("khw,dhw->kd", patches, back_two, preferred_element_type=f32).reshape(
            3, 3, inner, inner
        )
        * scale
    )
    back_taps = stacked_taps(pad_back, height, width, True)
    spatial_turned = jnp.transpose(w_spatial, (0, 1, 3, 2)).reshape(9 * inner, inner)
    back_pre = jnp.einsum("khw,kc->chw", back_taps, spatial_turned, preferred_element_type=f32)
    back_one = (back_pre * slope(pre_one)).astype(jnp.bfloat16)
    grad_reduce = jnp.einsum("chw,mhw->cm", feats, back_one, preferred_element_type=f32) * scale
    result = (
        jnp.einsum("mhw,cm->chw", back_one, w_reduce, preferred_element_type=f32) + top.astype(f32)
    ).astype(jnp.bfloat16)
    grad_reduce, grad_spatial, grad_expand = lax.psum(
        (grad_reduce, grad_spatial, grad_expand), ("dp", "row", "col")
    )
    return (result.reshape(1, channels, height, width), grad_reduce, grad_spatial, grad_expand)


def solution(mesh):
    in_specs = (P("dp", None, "row", "col"), P("dp", None, "row", "col"), P(), P(), P())
    out_specs = (P("dp", None, "row", "col"), P(), P(), P())
    return jax.shard_map(body, mesh=mesh, in_specs=in_specs, out_specs=out_specs, check_vma=False)
```

profile of v0, /device:TPU:8, one launch (start us, length us, event | category | flops | bytes accessed | tf_op | source)
XLA Modules:
  0.0 199.0 jit_solution(10238605451038991250)
XLA Ops:
  7.2 2.2 %copy.29 = bf16[256,24,128]{0,2,1:T(8,128)(2,1)S(1)} copy(bf16[256,24,128]{2,1,0:T(8,128)(2,1)} %bitcast.81) | data formatting | bytes 3145728 | tf_op jit(solution)/shard_map/squeeze | solution.py:47
  9.4 1.5 multiply_convert_fusion.1
  10.9 3.5 %collective-permute-start = (bf16[64,1,128]{2,0,1:T(8,128)(2,1)S(1)}, bf16[64,1,128]{2,0,1:T(8,128)(2,1)S(1)}, u32[]{:S(2)}, u32[]{:S(2)}) collective-permute-start(bf16[64,1,128]{2,0,1:T(8,128)(2,1)S(1)} %get-tuple-element.25), channel_id=1, source_target_pairs={{0,2},{2,4},{4,6},{1,3},{3,5},{5,7},{8,10},{10,12},{12,14},{9,11},... | collective-permute-start | bytes 49160 | tf_op jit(solution)/shard_map/ppermute | solution.py:15
  14.4 2.4 %collective-permute-start.1 = (bf16[64,1,128]{2,0,1:T(8,128)(2,1)S(1)}, bf16[64,1,128]{2,0,1:T(8,128)(2,1)S(1)}, u32[]{:S(2)}, u32[]{:S(2)}) collective-permute-start(bf16[64,1,128]{2,0,1:T(8,128)(2,1)S(1)} %get-tuple-element.26), channel_id=1, source_target_pairs={{2,0},{4,2},{6,4},{3,1},{5,3},{7,5},{10,8},{12,10},{14,12},{11,9},... | collective-permute-start | bytes 49160 | tf_op jit(solution)/shard_map/ppermute | solution.py:18
  16.7 3.3 %collective-permute-done.1 = bf16[64,1,128]{2,0,1:T(8,128)(2,1)S(1)} collective-permute-done((bf16[64,1,128]{2,0,1:T(8,128)(2,1)S(1)}, bf16[64,1,128]{2,0,1:T(8,128)(2,1)S(1)}, u32[]{:S(2)}, u32[]{:S(2)}) %collective-permute-start.1) | collective-permute-done | bytes 16416 | tf_op jit(solution)/shard_map/ppermute | solution.py:18
  21.1 1.3 collective-permute-start.2
  22.4 1.4 collective-permute-start.3
  23.8 2.9 %copy.19 = bf16[1,256,24,128]{1,3,2,0:T(8,128)(2,1)} copy(bf16[1,256,24,128]{3,2,1,0:T(8,128)(2,1)} %param.5) | data formatting | bytes 3145728 | tf_op args[0]
  26.7 2.8 %copy.18 = bf16[1,256,24,128]{1,3,2,0:T(8,128)(2,1)} copy(bf16[1,256,24,128]{3,2,1,0:T(8,128)(2,1)} %param.6) | data formatting | bytes 3145728 | tf_op args[1]
  33.6 2.7 %fusion.6 = bf16[256,24,128]{0,2,1:T(8,128)(2,1)S(1)} fusion(bf16[1,256,24,128]{1,3,2,0:T(8,128)(2,1)S(1)} %copy-done.4, bf16[1,256,24,128]{1,3,2,0:T(8,128)(2,1)S(1)} %copy-done.3, bf16[64,256]{1,0:T(8,128)(2,1)S(1)} %copy-done.9, f32[64,24,128]{2,0,1:T(8,128)S(1)} %convolution_bitcast_fusion.2), kind=kOutput, calls=%fused_computation.8 | convolution fusion | flops 119734272 | bytes 5537792 | tf_op jit(solution)/shard_map/mhw,mc->chw/dot_general | solution.py:61
  37.1 3.5 %collective-permute-start.4 = (bf16[64,1,128]{2,0,1:T(8,128)(2,1)S(1)}, bf16[64,1,128]{2,0,1:T(8,128)(2,1)S(1)}, u32[]{:S(2)}, u32[]{:S(2)}) collective-permute-start(bf16[64,1,128]{2,0,1:T(8,128)(2,1)S(1)} %get-tuple-element.23), channel_id=1, source_target_pairs={{0,2},{2,4},{4,6},{1,3},{3,5},{5,7},{8,10},{10,12},{12,14},{9,11},... | collective-permute-start | bytes 49160 | tf_op jit(solution)/shard_map/ppermute | solution.py:15
  40.6 2.4 %collective-permute-start.5 = (bf16[64,1,128]{2,0,1:T(8,128)(2,1)S(1)}, bf16[64,1,128]{2,0,1:T(8,128)(2,1)S(1)}, u32[]{:S(2)}, u32[]{:S(2)}) collective-permute-start(bf16[64,1,128]{2,0,1:T(8,128)(2,1)S(1)} %get-tuple-element.24), channel_id=1, source_target_pairs={{2,0},{4,2},{6,4},{3,1},{5,3},{7,5},{10,8},{12,10},{14,12},{11,9},... | collective-permute-start | bytes 49160 | tf_op jit(solution)/shard_map/ppermute | solution.py:18
  43.0 1.2 fusion.13
  44.2 2.2 %collective-permute-done.5 = bf16[64,1,128]{2,0,1:T(8,128)(2,1)S(1)} collective-permute-done((bf16[64,1,128]{2,0,1:T(8,128)(2,1)S(1)}, bf16[64,1,128]{2,0,1:T(8,128)(2,1)S(1)}, u32[]{:S(2)}, u32[]{:S(2)}) %collective-permute-start.5) | collective-permute-done | bytes 16416 | tf_op jit(solution)/shard_map/ppermute | solution.py:18
  47.3 1.3 collective-permute-start.6
  48.6 3.3 %collective-permute-start.7 = (bf16[64,26,1]{2,0,1:T(8,128)(2,1)S(1)}, bf16[64,26,1]{2,0,1:T(8,128)(2,1)S(1)}, u32[]{:S(2)}, u32[]{:S(2)}) collective-permute-start(bf16[64,26,1]{2,0,1:T(8,128)(2,1)S(1)} %get-tuple-element.17), channel_id=1, source_target_pairs={{0,1},{2,3},{4,5},{6,7},{8,9},{10,11},{12,13},{14,15},{16,17},{18,... | collective-permute-start | bytes 9992 | tf_op jit(solution)/shard_map/ppermute | solution.py:15
  51.9 1.1 fusion.14
  55.8 1.2 fusion.11
  58.0 1.6 fusion.8
  59.6 1.9 copy.28
  61.5 126.0 %all-reduce.3.cloned.1.call-done = (f32[256,64]{0,1:T(8,128)}, f32[3,3,64,64]{3,2,1,0:T(8,128)}, f32[64,256]{1,0:T(8,128)}) async-done(((f32[256,64]{0,1:T(8,128)}, f32[3,3,64,64]{3,2,1,0:T(8,128)}, f32[64,256]{1,0:T(8,128)}), (f32[256,64]{0,1:T(8,128)}, f32[3,3,64,64]{3,2,1,0:T(8,128)}, f32[64,256]{1,0:T(8,128)})) %all-reduce.3.cloned.1.call-update) | async-done | bytes 278544 | tf_op jit(solution)/shard_map/psum | solution.py:84
  187.5 1.5 copy.60
  188.9 1.7 copy.61
  190.6 1.5 copy.62
  (59 shorter events, 10.6 us)
Async XLA Ops:
  7.2 2.2 %copy-start = (bf16[256,64]{0,1:T(8,128)(2,1)S(1)}, bf16[256,64]{0,1:T(8,128)(2,1)}, u32[]{:S(2)}) copy-start(bf16[256,64]{0,1:T(8,128)(2,1)} %param.7) | copy-start | bytes 98308
  7.2 180.3 %all-reduce.3.cloned.1.call-start = ((), (), s32[]{:S(2)}) async-start(), calls=%async_computation | async-start | bytes 851968 | tf_op jit(solution)/shard_map/psum | solution.py:84
  10.9 5.8 %collective-permute-start = (bf16[64,1,128]{2,0,1:T(8,128)(2,1)S(1)}, bf16[64,1,128]{2,0,1:T(8,128)(2,1)S(1)}, u32[]{:S(2)}, u32[]{:S(2)}) collective-permute-start(bf16[64,1,128]{2,0,1:T(8,128)(2,1)S(1)} %get-tuple-element.25), channel_id=1, source_target_pairs={{0,2},{2,4},{4,6},{1,3},{3,5},{5,7},{8,10},{10,12},{12,14},{9,11},... | collective-permute-start | bytes 49160 | tf_op jit(solution)/shard_map/ppermute | solution.py:15
  14.4 5.6 %collective-permute-start.1 = (bf16[64,1,128]{2,0,1:T(8,128)(2,1)S(1)}, bf16[64,1,128]{2,0,1:T(8,128)(2,1)S(1)}, u32[]{:S(2)}, u32[]{:S(2)}) collective-permute-start(bf16[64,1,128]{2,0,1:T(8,128)(2,1)S(1)} %get-tuple-element.26), channel_id=1, source_target_pairs={{2,0},{4,2},{6,4},{3,1},{5,3},{7,5},{10,8},{12,10},{14,12},{11,9},... | collective-permute-start | bytes 49160 | tf_op jit(solution)/shard_map/ppermute | solution.py:18
  21.1 9.2 %collective-permute-start.2 = (bf16[64,26,1]{2,0,1:T(8,128)(2,1)}, bf16[64,26,1]{2,0,1:T(8,128)(2,1)S(1)}, u32[]{:S(2)}, u32[]{:S(2)}) collective-permute-start(bf16[64,26,1]{2,0,1:T(8,128)(2,1)} %get-tuple-element.22), channel_id=1, source_target_pairs={{0,1},{2,3},{4,5},{6,7},{8,9},{10,11},{12,13},{14,15},{16,17},{18,... | collective-permute-start | bytes 9992 | tf_op jit(solution)/shard_map/ppermute | solution.py:15
  22.4 7.1 %copy-start.7 = (bf16[3,3,64,64]{3,2,1,0:T(8,128)(2,1)S(1)}, bf16[3,3,64,64]{3,2,1,0:T(8,128)(2,1)}, u32[]{:S(2)}) copy-start(bf16[3,3,64,64]{3,2,1,0:T(8,128)(2,1)} %param.8) | copy-start | bytes 221188
  22.4 7.9 %collective-permute-start.3 = (bf16[64,26,1]{2,0,1:T(8,128)(2,1)S(1)}, bf16[64,26,1]{2,0,1:T(8,128)(2,1)S(1)}, u32[]{:S(2)}, u32[]{:S(2)}) collective-permute-start(bf16[64,26,1]{2,0,1:T(8,128)(2,1)S(1)} %get-tuple-element.21), channel_id=1, source_target_pairs={{1,0},{3,2},{5,4},{7,6},{9,8},{11,10},{13,12},{15,14},{17,16},{19,... | collective-permute-start | bytes 9992 | tf_op jit(solution)/shard_map/ppermute | solution.py:18
  31.7 1.4 copy-start.3
  31.7 1.9 copy-start.4
  31.8 1.9 copy-start.9
  36.4 15.5 %copy-start.1 = (bf16[256,24,128]{0,2,1:T(8,128)(2,1)}, bf16[256,24,128]{0,2,1:T(8,128)(2,1)S(1)}, u32[]{:S(2)}) copy-start(bf16[256,24,128]{0,2,1:T(8,128)(2,1)S(1)} %fusion.6) | copy-start | bytes 4718596
  37.1 7.0 %collective-permute-start.4 = (bf16[64,1,128]{2,0,1:T(8,128)(2,1)S(1)}, bf16[64,1,128]{2,0,1:T(8,128)(2,1)S(1)}, u32[]{:S(2)}, u32[]{:S(2)}) collective-permute-start(bf16[64,1,128]{2,0,1:T(8,128)(2,1)S(1)} %get-tuple-element.23), channel_id=1, source_target_pairs={{0,2},{2,4},{4,6},{1,3},{3,5},{5,7},{8,10},{10,12},{12,14},{9,11},... | collective-permute-start | bytes 49160 | tf_op jit(solution)/shard_map/ppermute | solution.py:15
  40.6 5.7 %collective-permute-start.5 = (bf16[64,1,128]{2,0,1:T(8,128)(2,1)S(1)}, bf16[64,1,128]{2,0,1:T(8,128)(2,1)S(1)}, u32[]{:S(2)}, u32[]{:S(2)}) collective-permute-start(bf16[64,1,128]{2,0,1:T(8,128)(2,1)S(1)} %get-tuple-element.24), channel_id=1, source_target_pairs={{2,0},{4,2},{6,4},{3,1},{5,3},{7,5},{10,8},{12,10},{14,12},{11,9},... | collective-permute-start | bytes 49160 | tf_op jit(solution)/shard_map/ppermute | solution.py:18
  47.3 6.5 %collective-permute-start.6 = (bf16[64,26,1]{2,0,1:T(8,128)(2,1)}, bf16[64,26,1]{2,0,1:T(8,128)(2,1)S(1)}, u32[]{:S(2)}, u32[]{:S(2)}) collective-permute-start(bf16[64,26,1]{2,0,1:T(8,128)(2,1)} %get-tuple-element.18), channel_id=1, source_target_pairs={{1,0},{3,2},{5,4},{7,6},{9,8},{11,10},{13,12},{15,14},{17,16},{19,... | collective-permute-start | bytes 9992 | tf_op jit(solution)/shard_map/ppermute | solution.py:18
  48.6 5.2 %collective-permute-start.7 = (bf16[64,26,1]{2,0,1:T(8,128)(2,1)S(1)}, bf16[64,26,1]{2,0,1:T(8,128)(2,1)S(1)}, u32[]{:S(2)}, u32[]{:S(2)}) collective-permute-start(bf16[64,26,1]{2,0,1:T(8,128)(2,1)S(1)} %get-tuple-element.17), channel_id=1, source_target_pairs={{0,1},{2,3},{4,5},{6,7},{8,9},{10,11},{12,13},{14,15},{16,17},{18,... | collective-permute-start | bytes 9992 | tf_op jit(solution)/shard_map/ppermute | solution.py:15
  54.6 1.1 copy-start.6
  54.6 1.1 copy-start.8
  55.8 2.2 %copy-start.2 = (bf16[256,24,128]{0,2,1:T(8,128)(2,1)S(1)}, bf16[256,24,128]{0,2,1:T(8,128)(2,1)}, u32[]{:S(2)}) copy-start(bf16[256,24,128]{0,2,1:T(8,128)(2,1)} %copy-done.1) | copy-start | bytes 4718596
  56.9 1.0 copy-start.5
Sparse Core Ops, SparseCore 0:
  58.1 129.3 all-reduce.2
where the time goes:
time: 199 us
  waiting for transfers between devices  131 us (66%)
  local copies, waits for them, and re-layouts  20.9 us (11%)
  starting transfers between devices  19 us (10%)
  between operations  14.4 us (7%)
  matrix products  11.8 us (6%)
    psum x1, waiting for transfers between devices, body(): lax.psum((grad_reduce, grad_spatial, grad_expand), ('dp', 'row', 'col'))  126 us
    unnamed x38, local copies, waits for them, and re-layouts  14.8 us
    ppermute x4, starting transfers between devices, padded_2(): lax.ppermute(lax.slice_in_dim(block, block.shape[dim] - width, None, axis...  11.5 us
    ppermute x4, starting transfers between devices, padded_2(): lax.ppermute(lax.slice_in_dim(block, 0, width, axis=dim), axis, backward)  7.41 us
    ppermute x4, waiting for transfers between devices, padded_2(): lax.ppermute(lax.slice_in_dim(block, 0, width, axis=dim), axis, backward)  5.42 us
  transfers between devices with their start and end apart: 9, of which 3 were waited for; matrix products, arithmetic and copies ran while one was open for 7% of the time, Pallas kernels for 0%

commit v1 on v0

--- a/solution.py
+++ b/solution.py
@@ -5,6 +5,11 @@
 
 GELU_C = 0.7978845608028654
 GELU_K = 0.044715
+
+
+def axis_by_axis(value, axis_one, axis_two):
+    partial = lax.psum(value, axis_one)
+    return lax.psum(partial, axis_two)
 
 
 def padded_2(block, sides, width):
@@ -81,8 +86,8 @@
     result = (
         jnp.einsum("mhw,cm->chw", back_one, w_reduce, preferred_element_type=f32) + top.astype(f32)
     ).astype(jnp.bfloat16)
-    grad_reduce, grad_spatial, grad_expand = lax.psum(
-        (grad_reduce, grad_spatial, grad_expand), ("dp", "row", "col")
+    grad_reduce, grad_spatial, grad_expand = axis_by_axis(
+        (grad_reduce, grad_spatial, grad_expand), "dp", ("row", "col")
     )
     return (result.reshape(1, channels, height, width), grad_reduce, grad_spatial, grad_expand)
 

time: 199 us -> 174 us (0.87)
  waiting for transfers between devices: 131 us -> 104 us
    psum x1 -> x2, waiting for transfers between devices: 126 us -> 98.7 us  [the longest x1 54.5 us: axis_by_axis(): return lax.psum(partial, axis_two)]
    unnamed x38 -> x34, local copies, waits for them, and re-layouts: 14.8 us -> 14.6 us
  transfers between devices with their start and end apart: 9 -> 10, of which waited for: 3 -> 4; matrix products, arithmetic and copies ran while one was open for 7% -> 7% of each run, Pallas kernels for 0% -> 0%
where the time goes in v1:
time: 174 us; the launch traced here: 173 us
  waiting for transfers between devices  104 us (60%)
  local copies, waits for them, and re-layouts  20.3 us (12%)
  starting transfers between devices  19.6 us (11%)
  between operations  14.4 us (8%)
  matrix products  11 us (6%)
  other arithmetic  3.41 us (2%)
    psum x1, waiting for transfers between devices, axis_by_axis(): return lax.psum(partial, axis_two)  54.5 us
    psum x1, waiting for transfers between devices, axis_by_axis(): partial = lax.psum(value, axis_one)  44.1 us
    unnamed x34, local copies, waits for them, and re-layouts  14.6 us
    ppermute x4, starting transfers between devices, padded_2(): lax.ppermute(lax.slice_in_dim(block, block.shape[dim] - width, None, axis...  12.1 us
    ppermute x4, starting transfers between devices, padded_2(): lax.ppermute(lax.slice_in_dim(block, 0, width, axis=dim), axis, backward)  7.41 us
    ppermute x4, waiting for transfers between devices, padded_2(): lax.ppermute(lax.slice_in_dim(block, 0, width, axis=dim), axis, backward)  5.35 us
  transfers between devices with their start and end apart: 10, of which 4 were waited for; matrix products, arithmetic and copies ran while one was open for 7% of the time, Pallas kernels for 0%

profile of v1, /device:TPU:8, one launch (start us, length us, event | category | flops | bytes accessed | tf_op | source)
XLA Modules:
  0.0 172.8 jit_solution(4859936067596511971)
XLA Ops:
  7.2 2.1 %copy.29 = bf16[256,24,128]{0,2,1:T(8,128)(2,1)S(1)} copy(bf16[256,24,128]{2,1,0:T(8,128)(2,1)} %bitcast.81) | data formatting | bytes 3145728 | tf_op jit(solution)/shard_map/squeeze | solution.py:52
  10.0 3.5 %collective-permute-start = (bf16[64,1,128]{2,0,1:T(8,128)(2,1)S(1)}, bf16[64,1,128]{2,0,1:T(8,128)(2,1)S(1)}, u32[]{:S(2)}, u32[]{:S(2)}) collective-permute-start(bf16[64,1,128]{2,0,1:T(8,128)(2,1)S(1)} %get-tuple-element.28), channel_id=1, source_target_pairs={{0,2},{2,4},{4,6},{1,3},{3,5},{5,7},{8,10},{10,12},{12,14},{9,11},... | collective-permute-start | bytes 49160 | tf_op jit(solution)/shard_map/ppermute | solution.py:20
  13.5 2.4 %collective-permute-start.1 = (bf16[64,1,128]{2,0,1:T(8,128)(2,1)S(1)}, bf16[64,1,128]{2,0,1:T(8,128)(2,1)S(1)}, u32[]{:S(2)}, u32[]{:S(2)}) collective-permute-start(bf16[64,1,128]{2,0,1:T(8,128)(2,1)S(1)} %get-tuple-element.29), channel_id=1, source_target_pairs={{2,0},{4,2},{6,4},{3,1},{5,3},{7,5},{10,8},{12,10},{14,12},{11,9},... | collective-permute-start | bytes 49160 | tf_op jit(solution)/shard_map/ppermute | solution.py:23
  15.9 3.3 %collective-permute-done.1 = bf16[64,1,128]{2,0,1:T(8,128)(2,1)S(1)} collective-permute-done((bf16[64,1,128]{2,0,1:T(8,128)(2,1)S(1)}, bf16[64,1,128]{2,0,1:T(8,128)(2,1)S(1)}, u32[]{:S(2)}, u32[]{:S(2)}) %collective-permute-start.1) | collective-permute-done | bytes 16416 | tf_op jit(solution)/shard_map/ppermute | solution.py:23
  20.3 1.3 collective-permute-start.2
  21.7 1.4 collective-permute-start.3
  23.1 2.9 %copy.19 = bf16[1,256,24,128]{1,3,2,0:T(8,128)(2,1)} copy(bf16[1,256,24,128]{3,2,1,0:T(8,128)(2,1)} %param.5) | data formatting | bytes 3145728 | tf_op args[0]
  26.0 2.8 %copy.18 = bf16[1,256,24,128]{1,3,2,0:T(8,128)(2,1)} copy(bf16[1,256,24,128]{3,2,1,0:T(8,128)(2,1)} %param.6) | data formatting | bytes 3145728 | tf_op args[1]
  28.9 1.5 pad_maximum_fusion
  33.2 2.7 %fusion.6 = bf16[256,24,128]{0,2,1:T(8,128)(2,1)S(1)} fusion(bf16[1,256,24,128]{1,3,2,0:T(8,128)(2,1)S(1)} %copy-done.4, bf16[1,256,24,128]{1,3,2,0:T(8,128)(2,1)S(1)} %copy-done.3, bf16[64,256]{1,0:T(8,128)(2,1)S(1)} %copy-done.7, f32[64,24,128]{2,0,1:T(8,128)S(1)} %convolution_bitcast_fusion.2), kind=kOutput, calls=%fused_computation.8 | convolution fusion | flops 119734272 | bytes 5537792 | tf_op jit(solution)/shard_map/mhw,mc->chw/dot_general | solution.py:66
  36.7 3.5 %collective-permute-start.4 = (bf16[64,1,128]{2,0,1:T(8,128)(2,1)S(1)}, bf16[64,1,128]{2,0,1:T(8,128)(2,1)S(1)}, u32[]{:S(2)}, u32[]{:S(2)}) collective-permute-start(bf16[64,1,128]{2,0,1:T(8,128)(2,1)S(1)} %get-tuple-element.26), channel_id=1, source_target_pairs={{0,2},{2,4},{4,6},{1,3},{3,5},{5,7},{8,10},{10,12},{12,14},{9,11},... | collective-permute-start | bytes 49160 | tf_op jit(solution)/shard_map/ppermute | solution.py:20
  40.2 2.4 %collective-permute-start.5 = (bf16[64,1,128]{2,0,1:T(8,128)(2,1)S(1)}, bf16[64,1,128]{2,0,1:T(8,128)(2,1)S(1)}, u32[]{:S(2)}, u32[]{:S(2)}) collective-permute-start(bf16[64,1,128]{2,0,1:T(8,128)(2,1)S(1)} %get-tuple-element.27), channel_id=1, source_target_pairs={{2,0},{4,2},{6,4},{3,1},{5,3},{7,5},{10,8},{12,10},{14,12},{11,9},... | collective-permute-start | bytes 49160 | tf_op jit(solution)/shard_map/ppermute | solution.py:23
  42.6 1.2 fusion.13
  43.8 2.1 %collective-permute-done.5 = bf16[64,1,128]{2,0,1:T(8,128)(2,1)S(1)} collective-permute-done((bf16[64,1,128]{2,0,1:T(8,128)(2,1)S(1)}, bf16[64,1,128]{2,0,1:T(8,128)(2,1)S(1)}, u32[]{:S(2)}, u32[]{:S(2)}) %collective-permute-start.5) | collective-permute-done | bytes 16416 | tf_op jit(solution)/shard_map/ppermute | solution.py:23
  47.0 1.3 collective-permute-start.6
  48.3 3.8 %collective-permute-start.7 = (bf16[64,26,1]{2,0,1:T(8,128)(2,1)}, bf16[64,26,1]{2,0,1:T(8,128)(2,1)}, u32[]{:S(2)}, u32[]{:S(2)}) collective-permute-start(bf16[64,26,1]{2,0,1:T(8,128)(2,1)} %get-tuple-element.20), channel_id=1, source_target_pairs={{0,1},{2,3},{4,5},{6,7},{8,9},{10,11},{12,13},{14,15},{16,17},{18,... | collective-permute-start | bytes 9992 | tf_op jit(solution)/shard_map/ppermute | solution.py:20
  54.1 1.5 maximum_maximum_fusion.1
  59.1 44.1 %all-reduce.7.cloned.1.call-done = (f32[256,64]{0,1:T(8,128)}, f32[3,3,64,64]{3,2,1,0:T(8,128)}, f32[64,256]{1,0:T(8,128)}) async-done(((f32[256,64]{0,1:T(8,128)}, f32[3,3,64,64]{3,2,1,0:T(8,128)}, f32[64,256]{1,0:T(8,128)}), (f32[256,64]{0,1:T(8,128)}, f32[3,3,64,64]{3,2,1,0:T(8,128)}, f32[64,256]{1,0:T(8,128)})) %all-reduce.7.cloned.1.call-update) | async-done | bytes 278544 | tf_op jit(solution)/shard_map/psum | solution.py:11
  103.2 1.6 fusion.8
  104.8 1.9 %copy.28 = bf16[1,256,24,128]{3,2,1,0:T(8,128)(2,1)} copy(bf16[1,256,24,128]{1,3,2,0:T(8,128)(2,1)S(1)} %fusion.8) | data formatting | bytes 3145728
  106.7 54.5 %all-reduce.5.cloned.1.call-done = (f32[256,64]{0,1:T(8,128)}, f32[3,3,64,64]{3,2,1,0:T(8,128)}, f32[64,256]{1,0:T(8,128)}) async-done(((f32[256,64]{0,1:T(8,128)}, f32[3,3,64,64]{3,2,1,0:T(8,128)}, f32[64,256]{1,0:T(8,128)}), (f32[256,64]{0,1:T(8,128)}, f32[3,3,64,64]{3,2,1,0:T(8,128)}, f32[64,256]{1,0:T(8,128)})) %all-reduce.5.cloned.1.call-update) | async-done | bytes 278544 | tf_op jit(solution)/shard_map/psum | solution.py:12
  161.3 1.5 copy.63
  162.8 1.7 copy.64
  164.5 1.5 copy.65
  (58 shorter events, 11.8 us)
Async XLA Ops:
  7.2 2.2 %copy-start = (bf16[256,64]{0,1:T(8,128)(2,1)S(1)}, bf16[256,64]{0,1:T(8,128)(2,1)}, u32[]{:S(2)}) copy-start(bf16[256,64]{0,1:T(8,128)(2,1)} %param.7) | copy-start | bytes 98308
  7.2 96.0 %all-reduce.7.cloned.1.call-start = ((), (), s32[]{:S(2)}) async-start(), calls=%async_computation.1 | async-start | bytes 851968 | tf_op jit(solution)/shard_map/psum | solution.py:11
  10.0 5.9 %collective-permute-start = (bf16[64,1,128]{2,0,1:T(8,128)(2,1)S(1)}, bf16[64,1,128]{2,0,1:T(8,128)(2,1)S(1)}, u32[]{:S(2)}, u32[]{:S(2)}) collective-permute-start(bf16[64,1,128]{2,0,1:T(8,128)(2,1)S(1)} %get-tuple-element.28), channel_id=1, source_target_pairs={{0,2},{2,4},{4,6},{1,3},{3,5},{5,7},{8,10},{10,12},{12,14},{9,11},... | collective-permute-start | bytes 49160 | tf_op jit(solution)/shard_map/ppermute | solution.py:20
  13.5 5.6 %collective-permute-start.1 = (bf16[64,1,128]{2,0,1:T(8,128)(2,1)S(1)}, bf16[64,1,128]{2,0,1:T(8,128)(2,1)S(1)}, u32[]{:S(2)}, u32[]{:S(2)}) collective-permute-start(bf16[64,1,128]{2,0,1:T(8,128)(2,1)S(1)} %get-tuple-element.29), channel_id=1, source_target_pairs={{2,0},{4,2},{6,4},{3,1},{5,3},{7,5},{10,8},{12,10},{14,12},{11,9},... | collective-permute-start | bytes 49160 | tf_op jit(solution)/shard_map/ppermute | solution.py:23
  20.3 8.6 %collective-permute-start.2 = (bf16[64,26,1]{2,0,1:T(8,128)(2,1)}, bf16[64,26,1]{2,0,1:T(8,128)(2,1)S(1)}, u32[]{:S(2)}, u32[]{:S(2)}) collective-permute-start(bf16[64,26,1]{2,0,1:T(8,128)(2,1)} %get-tuple-element.25), channel_id=1, source_target_pairs={{0,1},{2,3},{4,5},{6,7},{8,9},{10,11},{12,13},{14,15},{16,17},{18,... | collective-permute-start | bytes 9992 | tf_op jit(solution)/shard_map/ppermute | solution.py:20
  21.6 7.1 %copy-start.6 = (bf16[3,3,64,64]{3,2,1,0:T(8,128)(2,1)S(1)}, bf16[3,3,64,64]{3,2,1,0:T(8,128)(2,1)}, u32[]{:S(2)}) copy-start(bf16[3,3,64,64]{3,2,1,0:T(8,128)(2,1)} %param.8) | copy-start | bytes 221188
  21.7 7.3 %collective-permute-start.3 = (bf16[64,26,1]{2,0,1:T(8,128)(2,1)}, bf16[64,26,1]{2,0,1:T(8,128)(2,1)}, u32[]{:S(2)}, u32[]{:S(2)}) collective-permute-start(bf16[64,26,1]{2,0,1:T(8,128)(2,1)} %get-tuple-element.24), channel_id=1, source_target_pairs={{1,0},{3,2},{5,4},{7,6},{9,8},{11,10},{13,12},{15,14},{17,16},{19,... | collective-permute-start | bytes 9992 | tf_op jit(solution)/shard_map/ppermute | solution.py:23
  31.3 1.4 copy-start.3
  31.4 1.9 %copy-start.4 = (bf16[1,256,24,128]{1,3,2,0:T(8,128)(2,1)S(1)}, bf16[1,256,24,128]{1,3,2,0:T(8,128)(2,1)}, u32[]{:S(2)}) copy-start(bf16[1,256,24,128]{1,3,2,0:T(8,128)(2,1)} %copy.18) | copy-start | bytes 4718596
  31.4 1.9 %copy-start.7 = (bf16[64,256]{1,0:T(8,128)(2,1)S(1)}, bf16[64,256]{1,0:T(8,128)(2,1)}, u32[]{:S(2)}) copy-start(bf16[64,256]{1,0:T(8,128)(2,1)} %param.9) | copy-start | bytes 98308
  36.0 16.2 %copy-start.1 = (bf16[256,24,128]{0,2,1:T(8,128)(2,1)}, bf16[256,24,128]{0,2,1:T(8,128)(2,1)S(1)}, u32[]{:S(2)}) copy-start(bf16[256,24,128]{0,2,1:T(8,128)(2,1)S(1)} %fusion.6) | copy-start | bytes 4718596
  36.7 7.0 %collective-permute-start.4 = (bf16[64,1,128]{2,0,1:T(8,128)(2,1)S(1)}, bf16[64,1,128]{2,0,1:T(8,128)(2,1)S(1)}, u32[]{:S(2)}, u32[]{:S(2)}) collective-permute-start(bf16[64,1,128]{2,0,1:T(8,128)(2,1)S(1)} %get-tuple-element.26), channel_id=1, source_target_pairs={{0,2},{2,4},{4,6},{1,3},{3,5},{5,7},{8,10},{10,12},{12,14},{9,11},... | collective-permute-start | bytes 49160 | tf_op jit(solution)/shard_map/ppermute | solution.py:20
  40.2 5.6 %collective-permute-start.5 = (bf16[64,1,128]{2,0,1:T(8,128)(2,1)S(1)}, bf16[64,1,128]{2,0,1:T(8,128)(2,1)S(1)}, u32[]{:S(2)}, u32[]{:S(2)}) collective-permute-start(bf16[64,1,128]{2,0,1:T(8,128)(2,1)S(1)} %get-tuple-element.27), channel_id=1, source_target_pairs={{2,0},{4,2},{6,4},{3,1},{5,3},{7,5},{10,8},{12,10},{14,12},{11,9},... | collective-permute-start | bytes 49160 | tf_op jit(solution)/shard_map/ppermute | solution.py:23
  47.0 7.1 %collective-permute-start.6 = (bf16[64,26,1]{2,0,1:T(8,128)(2,1)}, bf16[64,26,1]{2,0,1:T(8,128)(2,1)S(1)}, u32[]{:S(2)}, u32[]{:S(2)}) collective-permute-start(bf16[64,26,1]{2,0,1:T(8,128)(2,1)} %get-tuple-element.21), channel_id=1, source_target_pairs={{1,0},{3,2},{5,4},{7,6},{9,8},{11,10},{13,12},{15,14},{17,16},{19,... | collective-permute-start | bytes 9992 | tf_op jit(solution)/shard_map/ppermute | solution.py:23
  48.3 5.8 %collective-permute-start.7 = (bf16[64,26,1]{2,0,1:T(8,128)(2,1)}, bf16[64,26,1]{2,0,1:T(8,128)(2,1)}, u32[]{:S(2)}, u32[]{:S(2)}) collective-permute-start(bf16[64,26,1]{2,0,1:T(8,128)(2,1)} %get-tuple-element.20), channel_id=1, source_target_pairs={{0,1},{2,3},{4,5},{6,7},{8,9},{10,11},{12,13},{14,15},{16,17},{18,... | collective-permute-start | bytes 9992 | tf_op jit(solution)/shard_map/ppermute | solution.py:20
  57.9 1.1 copy-start.5
  57.9 45.3 %copy-start.2 = (bf16[256,24,128]{0,2,1:T(8,128)(2,1)S(1)}, bf16[256,24,128]{0,2,1:T(8,128)(2,1)}, u32[]{:S(2)}) copy-start(bf16[256,24,128]{0,2,1:T(8,128)(2,1)} %copy-done.1) | copy-start | bytes 4718596
  59.0 102.3 %all-reduce.5.cloned.1.call-start = ((), (), s32[]{:S(2)}) async-start(), calls=%async_computation | async-start | bytes 851968 | tf_op jit(solution)/shard_map/psum | solution.py:12
Sparse Core Ops, SparseCore 0:
  59.1 44.0 all-reduce.6
  105.7 55.5 all-reduce.4
